TPU v7x, 512 devices: a whole 4x4x16 slice. The times are simulated.
512 devices in a mesh: batch: 64 (over z, y_hi, core), coef: 8 (over y_lo, x).
Axes of the slice: x: 4, y: 4 (y_hi: 2, y_lo: 2; y = y_hi * 2 + y_lo), z: 16, core: 2. Of those that a mesh axis runs over, the one named last changes fastest.
Arguments:
- jac_blocks: bfloat16 [2048, 8, 2, 128, 128], P(('batch', 'coef')), may hold values from -0.52734375 to 0.52734375
- col_blocks: int32 [8, 2048, 2], P('coef', 'batch'), may hold values from 0 to 63, all different within a row; in each aligned block of 32 rows (0 to 31, 32 to 63, ..., all dimensions but the last counted through in order) at most 2 rows name the same one
- residual: float32 [2048, 128], P('batch'), may hold values from -6 to 6
- run_of_half: int32 [4096], P('batch'), may hold values from 0 to 4095, each once
- run_scale: bfloat16 [4096], replicated, may hold values from 0.25 to 4
Outputs:
- diag_blocks: float32 [8, 64, 128, 128], P('coef', 'batch')
- gradient: float32 [8, 64, 128], P('coef', 'batch')
Inputs may be any that keep to these rules, and one draw needn't show every extreme that they name: `col_blocks`: the 2 column blocks of one row block in one group differ. For each group, among the row blocks of one batch index (aligned blocks of the row-block dimension), no column block is named more than 2 times, a bound that some block reaches. `run_of_half`: every run appears exactly once.
All inputs are finite; a program needn't handle non-finite values.
Results may differ from a plain program's by a relative error of at most 0.00043.
Values may be sent and summed in bfloat16 or wider, within the bound.
No kernel may reach another device: no remote copies, remote signals or barrier semaphores. Data moves between devices by JAX's collectives and lax.ppermute only.
A program may use at most 64 MiB of HBM per device.

v0:
```python
import jax
import jax.numpy as jnp
from jax import lax
from jax.sharding import PartitionSpec as P

BS = 128
PAIR = 2


def shards(jac_blocks, col_blocks, residual, run_of_half, run_scale):
    width = lax.axis_size("batch")
    myself = lax.axis_index("batch")
    moved = lax.all_to_all(jac_blocks, "coef", split_axis=1, concat_axis=0, tiled=True)
    items = moved.reshape(-1, BS, BS)
    targets = col_blocks.reshape(-1)
    scale_rows = run_scale.astype(jnp.float32)[run_of_half].reshape(-1, 2)
    weights = jnp.repeat(scale_rows, BS // 2, axis=1)
    item_w = jnp.repeat(weights, PAIR, axis=0)
    item_res = jnp.repeat(residual, PAIR, axis=0)
    onehot = (targets[:, None] == jnp.arange(width, dtype=jnp.int32)[None, :]).astype(jnp.float32)
    gterms = jnp.einsum(
        "iak,ia->ik", items.astype(jnp.float32), item_w * item_res, precision=lax.Precision.HIGHEST
    )
    gpart = jnp.einsum("il,ik->lk", onehot, gterms, precision=lax.Precision.HIGHEST)
    gtotal = lax.psum(gpart, "batch")
    gradient = lax.dynamic_slice_in_dim(gtotal, myself, 1, 0).reshape(1, 1, BS)
    weighted = (items.astype(jnp.float32) * item_w[:, :, None]).astype(jnp.bfloat16)
    products = lax.dot_general(
        items, weighted, (((1,), (1,)), ((0,), (0,))), preferred_element_type=jnp.float32
    )
    diag = lax.psum_scatter(
        jnp.einsum("il,ikb->lkb", onehot, products, precision=lax.Precision.HIGHEST),
        "batch",
        scatter_dimension=0,
        tiled=True,
    )
    return (diag.reshape(1, 1, BS, BS), gradient)


def solution(mesh):
    in_specs = (
        P(("batch", "coef"), None, None, None, None),
        P("coef", "batch", None),
        P("batch", None),
        P("batch"),
        P(),
    )
    out_specs = (P("coef", "batch", None, None), P("coef", "batch", None))
    return jax.shard_map(shards, mesh=mesh, in_specs=in_specs, out_specs=out_specs, check_vma=False)
```

profile of v0, /device:TPU:6, one launch (start us, length us, event | category | flops | bytes accessed | tf_op | source)
XLA Modules:
  0.0 338.0 jit_solution(15510032029880882865)
XLA Ops:
  7.2 0.0 copy-start.2
  7.2 0.0 copy-start.1
  7.2 0.0 copy-start.3
  7.2 3.2 copy.11
  10.4 9.4 %all-to-all-start = ((bf16[4,8,2,128,128]{4,3,2,0,1:T(8,128)(2,1)}), bf16[4,8,2,128,128]{4,3,2,0,1:T(8,128)(2,1)S(1)}, u32[]{:S(2)}, u32[]{:S(2)}) async-start(bf16[4,8,2,128,128]{4,3,2,0,1:T(8,128)(2,1)} %copy.11), calls=%async_computation | async-start | bytes 4194304 | tf_op jit(solution)/shard_map/all_to_all | solution.py:13
  19.8 0.0 reduce-scatter.2.cloned.1.call-start
  19.8 0.0 copy-done.2
  19.8 0.1 copy.10
  19.8 0.1 eq.15
  20.0 0.0 copy-done.1
  20.0 0.0 copy-done.3
  20.0 0.8 gather_fusion
  20.8 0.1 reshape.27
  20.9 0.1 broadcast_in_dim.14
  21.0 0.1 reshape.28
  21.1 20.6 %all-to-all-done = bf16[4,8,2,128,128]{4,3,2,0,1:T(8,128)(2,1)S(1)} async-done(((bf16[4,8,2,128,128]{4,3,2,0,1:T(8,128)(2,1)}), bf16[4,8,2,128,128]{4,3,2,0,1:T(8,128)(2,1)S(1)}, u32[]{:S(2)}, u32[]{:S(2)}) %all-to-all-start) | async-done | bytes 2097184 | tf_op jit(solution)/shard_map/all_to_all | solution.py:13
  41.7 4.2 %fusion.1 = f32[64,128,128]{1,2,0:T(8,128)} fusion(bf16[64,128,128]{2,1,0:T(8,128)(2,1)S(1)} %bitcast.25, f32[64,128]{1,0:T(8,128)S(1)} %bitcast.27), kind=kOutput, calls=%fused_computation.3 | convolution fusion | flops 271581184 | bytes 6324224 | tf_op jit(solution)/shard_map/dot_general | solution.py:28
  45.8 5.4 %copy.13 = f32[64,128,128]{2,0,1:T(8,128)} copy(f32[64,128,128]{1,2,0:T(8,128)} %fusion.1) | data formatting | bytes 8388608 | tf_op jit(solution)/shard_map/dot_general | solution.py:28
  51.2 4.6 %fusion.5 = f32[64,128,128]{2,0,1:T(8,128)S(1)} fusion(f32[64,128,128]{2,0,1:T(8,128)} %copy.13, s32[64]{0:T(128)S(1)} %eq.15), kind=kOutput, calls=%fused_computation.8 | convolution fusion | flops 805310464 | bytes 8388864 | tf_op jit(solution)/shard_map/il,ikb->lkb/dot_general | solution.py:32
  55.8 4.4 %copy.14 = f32[64,128,128]{2,1,0:T(8,128)} copy(f32[64,128,128]{2,0,1:T(8,128)S(1)} %fusion.5) | data formatting | bytes 8388608 | tf_op jit(solution)/shard_map/il,ikb->lkb/dot_general | solution.py:32
  60.2 0.0 copy-start
  60.2 0.0 reduce-scatter.2.cloned.1.call-update
  60.2 0.7 copy-done
  60.9 1.7 fusion.9
  62.7 0.1 fusion.3
  62.8 267.8 %psum.7 = f32[64,128]{1,0:T(8,128)S(1)} all-reduce(f32[64,128]{1,0:T(8,128)S(1)} %fusion.3), channel_id=1, replica_groups=mesh['batch'=64,'coef'=8] {'batch'}, use_global_device_ids=true, to_apply=%region_1.0 | all-reduce | flops 8192 | bytes 65536 | tf_op jit(solution)/shard_map/psum | solution.py:25
  330.7 0.5 dynamic-slice_bitcast_fusion
  331.2 0.0 reduce-scatter.2.cloned.1.call-done
  (6 shorter events, 0.0 us)
Async XLA Ops:
  7.2 12.6 %copy-start.2 = (s32[1,32,2]{1,2,0:T(2,128)S(1)}, s32[1,32,2]{1,2,0:T(2,128)}, u32[]{:S(2)}) copy-start(s32[1,32,2]{1,2,0:T(2,128)} %param.6) | copy-start | bytes 772
  7.2 12.8 %copy-start.1 = (bf16[4096]{0:T(1024)(128)(2,1)S(1)}, bf16[4096]{0:T(1024)(128)(2,1)}, u32[]{:S(2)}) copy-start(bf16[4096]{0:T(1024)(128)(2,1)} %param.9) | copy-start | bytes 24580
  7.2 12.8 %copy-start.3 = (s32[64]{0:T(128)S(1)}, s32[64]{0:T(128)}, u32[]{:S(2)}) copy-start(s32[64]{0:T(128)} %param.8) | copy-start | bytes 772
  10.4 31.3 %all-to-all-start = ((bf16[4,8,2,128,128]{4,3,2,0,1:T(8,128)(2,1)}), bf16[4,8,2,128,128]{4,3,2,0,1:T(8,128)(2,1)S(1)}, u32[]{:S(2)}, u32[]{:S(2)}) async-start(bf16[4,8,2,128,128]{4,3,2,0,1:T(8,128)(2,1)} %copy.11), calls=%async_computation | async-start | bytes 4194304 | tf_op jit(solution)/shard_map/all_to_all | solution.py:13
  19.8 311.4 %reduce-scatter.2.cloned.1.call-start = ((), (), s32[]{:S(2)}) async-start(), calls=%async_computation.2 | async-start | bytes 4259840 | tf_op jit(solution)/shard_map/reduce_scatter | solution.py:31
  60.2 0.7 copy-start
Sparse Core Ops, SparseCore 0:
  60.3 228.2 reduce-scatter.1
where the time goes:
time: 338 us
  blocking collectives  268 us (79%)
  waiting for transfers between devices  20.6 us (6%)
  local copies, waits for them, and re-layouts  15.5 us (5%)
  between operations  14.1 us (4%)
  matrix products  10.6 us (3%)
  starting transfers between devices  9.37 us (3%)
    psum x1, blocking collectives, shards(): gtotal = lax.psum(gpart, 'batch')  268 us
    all_to_all x1, waiting for transfers between devices, shards(): lax.all_to_all(jac_blocks, 'coef', split_axis=1, concat_axis=0, tiled=True)  20.6 us
    all_to_all x1, starting transfers between devices, shards(): lax.all_to_all(jac_blocks, 'coef', split_axis=1, concat_axis=0, tiled=True)  9.37 us
  transfers between devices with their start and end apart: 2, of which 1 were waited for; matrix products, arithmetic and copies ran while one was open for 1% of the time, Pallas kernels for 0%

commit v1 on v0

--- a/solution.py
+++ b/solution.py
@@ -1,3 +1,4 @@
+import functools
 import jax
 import jax.numpy as jnp
 from jax import lax
@@ -5,6 +6,13 @@
 
 BS = 128
 PAIR = 2
+
+
+def layers_all_start(sheet, device_axis):
+    return jnp.sum(lax.all_gather(sheet, device_axis), axis=0)
+
+
+raise_zone = functools.partial(layers_all_start, device_axis="batch")
 
 
 def shards(jac_blocks, col_blocks, residual, run_of_half, run_scale):
@@ -22,7 +30,7 @@
         "iak,ia->ik", items.astype(jnp.float32), item_w * item_res, precision=lax.Precision.HIGHEST
     )
     gpart = jnp.einsum("il,ik->lk", onehot, gterms, precision=lax.Precision.HIGHEST)
-    gtotal = lax.psum(gpart, "batch")
+    gtotal = raise_zone(gpart)
     gradient = lax.dynamic_slice_in_dim(gtotal, myself, 1, 0).reshape(1, 1, BS)
     weighted = (items.astype(jnp.float32) * item_w[:, :, None]).astype(jnp.bfloat16)
     products = lax.dot_general(

time: 338 us -> 423 us (1.25)
  waiting for transfers between devices: 20.6 us -> 371 us
  blocking collectives: 268 us -> 0 us
    psum x1 -> x0, blocking collectives: 268 us -> none  [shards(): gtotal = lax.psum(gpart, 'batch')]
    reduce_scatter x1, waiting for transfers between devices: 0.01 us -> 219 us  [shards(): lax.psum_scatter(jnp.einsum('il,ikb->lkb', onehot, products, precision=la...]
    all_gather x0 -> x1, waiting for transfers between devices: none -> 131 us  [layers_all_start(): return jnp.sum(lax.all_gather(sheet, device_axis), axis=0)]
  transfers between devices with their start and end apart: 2 -> 3, of which waited for: 1 -> 3; matrix products, arithmetic and copies ran while one was open for 1% -> 5% of each run, Pallas kernels for 0% -> 0%
where the time goes in v1:
time: 423 us
  waiting for transfers between devices  371 us (88%)
  local copies, waits for them, and re-layouts  14.8 us (3%)
  between operations  14.1 us (3%)
  matrix products  11.2 us (3%)
  starting transfers between devices  9.56 us (2%)
    reduce_scatter x1, waiting for transfers between devices, shards(): lax.psum_scatter(jnp.einsum('il,ikb->lkb', onehot, products, precision=la...  219 us
    all_gather x1, waiting for transfers between devices, layers_all_start(): return jnp.sum(lax.all_gather(sheet, device_axis), axis=0)  131 us
    all_to_all x1, waiting for transfers between devices, shards(): lax.all_to_all(jac_blocks, 'coef', split_axis=1, concat_axis=0, tiled=True)  20.5 us
    all_to_all x1, starting transfers between devices, shards(): lax.all_to_all(jac_blocks, 'coef', split_axis=1, concat_axis=0, tiled=True)  9.51 us
  transfers between devices with their start and end apart: 3, of which 3 were waited for; matrix products, arithmetic and copies ran while one was open for 5% of the time, Pallas kernels for 0%

profile of v1, /device:TPU:6, one launch (start us, length us, event | category | flops | bytes accessed | tf_op | source)
XLA Modules:
  0.0 422.6 jit_solution(3361974276298030179)
XLA Ops:
  7.2 3.2 copy.11
  10.4 0.0 copy-start.2
  10.4 0.0 copy-start.1
  10.4 0.0 copy-start.3
  10.4 0.0 copy-start
  10.4 9.5 %all-to-all-start = ((bf16[4,8,2,128,128]{4,3,2,0,1:T(8,128)(2,1)}), bf16[4,8,2,128,128]{4,3,2,0,1:T(8,128)(2,1)S(1)}, u32[]{:S(2)}, u32[]{:S(2)}) async-start(bf16[4,8,2,128,128]{4,3,2,0,1:T(8,128)(2,1)} %copy.11), calls=%async_computation | async-start | bytes 4194304 | tf_op jit(solution)/shard_map/all_to_all | solution.py:21
  19.9 0.0 all-gather.3.cloned.1.call-start
  19.9 0.0 copy-done.2
  19.9 0.1 copy.10
  20.0 0.1 eq.15
  20.1 0.0 copy-done.1
  20.1 0.0 copy-done.3
  20.1 0.8 gather_fusion
  20.9 0.1 reshape.27
  21.0 0.1 broadcast_in_dim.14
  21.1 0.1 reshape.28
  21.2 0.0 copy-done
  21.3 20.5 %all-to-all-done = bf16[4,8,2,128,128]{4,3,2,0,1:T(8,128)(2,1)S(1)} async-done(((bf16[4,8,2,128,128]{4,3,2,0,1:T(8,128)(2,1)}), bf16[4,8,2,128,128]{4,3,2,0,1:T(8,128)(2,1)S(1)}, u32[]{:S(2)}, u32[]{:S(2)}) %all-to-all-start) | async-done | bytes 2097184 | tf_op jit(solution)/shard_map/all_to_all | solution.py:21
  41.8 1.7 fusion.9
  43.5 0.8 fusion.3
  44.3 0.0 all-gather.3.cloned.1.call-update
  44.3 0.0 reduce-scatter.2.cloned.1.call-start
  44.4 4.1 fusion.1
  48.5 5.4 %copy.13 = f32[64,128,128]{2,0,1:T(8,128)} copy(f32[64,128,128]{1,2,0:T(8,128)} %fusion.1) | data formatting | bytes 8388608 | tf_op jit(solution)/shard_map/dot_general | solution.py:36
  53.9 4.6 %fusion.5 = f32[64,128,128]{2,0,1:T(8,128)S(1)} fusion(f32[64,128,128]{2,0,1:T(8,128)} %copy.13, s32[64]{0:T(128)S(1)} %eq.15), kind=kOutput, calls=%fused_computation.8 | convolution fusion | flops 805310464 | bytes 8388864 | tf_op jit(solution)/shard_map/il,ikb->lkb/dot_general | solution.py:40
  58.5 4.4 %copy.14 = f32[64,128,128]{2,1,0:T(8,128)} copy(f32[64,128,128]{2,0,1:T(8,128)S(1)} %fusion.5) | data formatting | bytes 8388608 | tf_op jit(solution)/shard_map/il,ikb->lkb/dot_general | solution.py:40
  62.9 0.0 reduce-scatter.2.cloned.1.call-update
  62.9 131.1 %all-gather.3.cloned.1.call-done = f32[4096,128]{1,0:T(8,128)} async-done(((f32[64,128]{1,0:T(8,128)}), f32[4096,128]{1,0:T(8,128)}) %all-gather.3.cloned.1.call-update) | async-done | bytes 2097168 | tf_op jit(solution)/shard_map/all_gather | solution.py:12
  194.0 1.7 reduce_sum.9
  195.8 0.5 dynamic-slice_bitcast_fusion
  196.3 219.5 %reduce-scatter.2.cloned.1.call-done = f32[1,128,128]{2,1,0:T(8,128)} async-done(((f32[64,128,128]{2,1,0:T(8,128)}), f32[1,128,128]{2,1,0:T(8,128)}) %reduce-scatter.2.cloned.1.call-update) | async-done | bytes 65552 | tf_op jit(solution)/shard_map/reduce_scatter | solution.py:39
  (6 shorter events, 0.0 us)
Async XLA Ops:
  10.4 9.5 %copy-start.2 = (s32[1,32,2]{1,2,0:T(2,128)S(1)}, s32[1,32,2]{1,2,0:T(2,128)}, u32[]{:S(2)}) copy-start(s32[1,32,2]{1,2,0:T(2,128)} %param.6) | copy-start | bytes 772
  10.4 9.7 %copy-start.1 = (bf16[4096]{0:T(1024)(128)(2,1)S(1)}, bf16[4096]{0:T(1024)(128)(2,1)}, u32[]{:S(2)}) copy-start(bf16[4096]{0:T(1024)(128)(2,1)} %param.9) | copy-start | bytes 24580
  10.4 9.7 %copy-start.3 = (s32[64]{0:T(128)S(1)}, s32[64]{0:T(128)}, u32[]{:S(2)}) copy-start(s32[64]{0:T(128)} %param.8) | copy-start | bytes 772
  10.4 10.9 %copy-start = (f32[32,128]{1,0:T(8,128)S(1)}, f32[32,128]{1,0:T(8,128)}, u32[]{:S(2)}) copy-start(f32[32,128]{1,0:T(8,128)} %param.7) | copy-start | bytes 49156
  10.4 31.4 %all-to-all-start = ((bf16[4,8,2,128,128]{4,3,2,0,1:T(8,128)(2,1)}), bf16[4,8,2,128,128]{4,3,2,0,1:T(8,128)(2,1)S(1)}, u32[]{:S(2)}, u32[]{:S(2)}) async-start(bf16[4,8,2,128,128]{4,3,2,0,1:T(8,128)(2,1)} %copy.11), calls=%async_computation | async-start | bytes 4194304 | tf_op jit(solution)/shard_map/all_to_all | solution.py:21
  19.9 174.2 %all-gather.3.cloned.1.call-start = ((), (), s32[]{:S(2)}) async-start(), calls=%async_computation.3 | async-start | bytes 2129920 | tf_op jit(solution)/shard_map/all_gather | solution.py:12
  44.3 371.5 %reduce-scatter.2.cloned.1.call-start = ((), (), s32[]{:S(2)}) async-start(), calls=%async_computation.2 | async-start | bytes 4259840 | tf_op jit(solution)/shard_map/reduce_scatter | solution.py:39
Sparse Core Ops, SparseCore 0:
  44.4 149.5 all-gather.2
  199.3 216.4 reduce-scatter.1
